TPU v7x, 32 devices: a whole 2x2x4 slice. The times are simulated.
32 devices in a mesh: row: 8 (over z, core), col: 4 (over y, x).
Axes of the slice: x: 2, y: 2, z: 4, core: 2. Of those that a mesh axis runs over, the one named last changes fastest.
Arguments:
- features: bfloat16 [9, 1, 128, 128, 128], P(None, None, 'row', 'col'), may hold values from -12 to 12
- cotangent: float32 [3, 1, 128, 128, 128], P(None, None, 'row', 'col'), may hold values from -14 to 14
- w_in: bfloat16 [9, 256], replicated, may hold values from -2 to 2
- bias_in: float32 [256], replicated, may hold values from -3 to 3
- w_mid: bfloat16 [256, 256], replicated, may hold values from -0.375 to 0.375
- bias_mid: float32 [256], replicated, may hold values from -3 to 3
- w_out: bfloat16 [256, 6], replicated, may hold values from -2.5 to 2.5
Outputs:
- grad_features: float32 [9, 1, 128, 128, 128], P(None, None, 'row', 'col')
- grad_w_in: float32 [9, 256], replicated
- grad_b_in: float32 [256], replicated
- grad_w_mid: float32 [256, 256], replicated
- grad_b_mid: float32 [256], replicated
- grad_w_out: float32 [256, 6], replicated
All inputs are finite; a program needn't handle non-finite values.
Results may differ from a plain program's by a relative error of at most 0.025.
Values sent between devices are 32-bit elements; how exact they have to be, the bound alone decides.
A program may use at most 128 MiB of HBM per device.

v0:
```python
import math
import jax
import jax.numpy as jnp
from jax import lax
from jax.sharding import PartitionSpec as P

NX = 128
NY = 128
NZ = 128
CELLS = 2097152
STEP_DT = 0.04
PAIRS = ((0, 0), (1, 1), (2, 2), (0, 1), (0, 2), (1, 2))


def mode_list(count, length):
    index = jnp.arange(count, dtype=jnp.int32)
    return jnp.where(index < length // 2, index, index - length)


def phase_table(modes, length):
    positions = jnp.arange(length, dtype=jnp.int32)
    turns = positions[:, None] * modes[None, :] % length
    angle = turns.astype(jnp.float32) * (2.0 * math.pi / length)
    return (jnp.cos(angle), jnp.sin(angle))


def contract(form, left, right):
    return jnp.einsum(
        form, left, right, precision=lax.Precision.HIGHEST, preferred_element_type=jnp.float32
    )


def complex_product(form, part, table_real, table_imag):
    real = contract(form, part[0], table_real) - contract(form, part[1], table_imag)
    imag = contract(form, part[0], table_imag) + contract(form, part[1], table_real)
    return jnp.stack([real, imag])


def closure_block(x_blk, g_blk, w_in, bias_in, w_mid, bias_mid, w_out):
    pre_in = (
        jnp.einsum("fh,fn->hn", w_in, x_blk, preferred_element_type=jnp.float32) + bias_in[:, None]
    )
    act_in = jnp.tanh(pre_in).astype(jnp.bfloat16)
    pre_mid = (
        jnp.einsum("io,in->on", w_mid, act_in, preferred_element_type=jnp.float32)
        + bias_mid[:, None]
    )
    act_mid = jnp.tanh(pre_mid).astype(jnp.bfloat16)
    back_mid = jnp.einsum("ho,on->hn", w_out, g_blk, preferred_element_type=jnp.float32)
    delta_mid = (back_mid * (1.0 - jnp.square(act_mid.astype(jnp.float32)))).astype(jnp.bfloat16)
    back_in = jnp.einsum("io,on->in", w_mid, delta_mid, preferred_element_type=jnp.float32)
    delta_in = (back_in * (1.0 - jnp.square(act_in.astype(jnp.float32)))).astype(jnp.bfloat16)
    grad_x = jnp.einsum("fh,hn->fn", w_in, delta_in, preferred_element_type=jnp.float32)
    gw_out = jnp.einsum("hn,on->ho", act_mid, g_blk, preferred_element_type=jnp.float32)
    gw_mid = jnp.einsum("in,on->io", act_in, delta_mid, preferred_element_type=jnp.float32)
    gw_in = jnp.einsum("fn,hn->fh", x_blk, delta_in, preferred_element_type=jnp.float32)
    gb_mid = jnp.sum(delta_mid.astype(jnp.float32), axis=1)
    gb_in = jnp.sum(delta_in.astype(jnp.float32), axis=1)
    return (grad_x, (gw_in, gb_in, gw_mid, gb_mid, gw_out))


def per_device(features, cotangent, w_in, bias_in, w_mid, bias_mid, w_out):
    rows_group = lax.axis_size("row")
    cols_group = lax.axis_size("col")
    count_y = NY
    count_z = NZ
    list_z = mode_list(count_z, NZ)
    weight_z = jnp.ones((count_z,), jnp.float32) / NZ
    list_x = mode_list(NX, NX)
    list_y = mode_list(count_y, NY)
    cos_x, sin_x = phase_table(list_x, NX)
    cos_y, sin_y = phase_table(list_y, NY)
    cos_z, sin_z = phase_table(list_z, NZ)
    forward_z = jnp.stack(
        [
            contract("csxyz,zk->csxky", cotangent, cos_z),
            -contract("csxyz,zk->csxky", cotangent, sin_z),
        ]
    )
    spectra = complex_product(
        "csxky,yq->cskqx",
        lax.all_to_all(forward_z, "col", split_axis=4, concat_axis=5, tiled=True),
        cos_y,
        -sin_y,
    )
    spectra = complex_product(
        "cskqx,xp->cskqp",
        lax.all_to_all(spectra, "row", split_axis=4, concat_axis=5, tiled=True),
        cos_x,
        -sin_x,
    )
    share_y = count_y // rows_group
    share_z = count_z // cols_group
    local_y = lax.dynamic_slice_in_dim(list_y, lax.axis_index("row") * share_y, share_y)
    local_z = lax.dynamic_slice_in_dim(list_z, lax.axis_index("col") * share_z, share_z)
    modes_x = list_x[None, None, :]
    modes_y = local_y[None, :, None]
    modes_z = local_z[:, None, None]
    keep = (3 * jnp.abs(modes_x) < NX) & (3 * jnp.abs(modes_y) < NY) & (3 * jnp.abs(modes_z) < NZ)
    waves = [modes_x.astype(jnp.float32), modes_y.astype(jnp.float32), modes_z.astype(jnp.float32)]
    velocity = [spectra[:, comp] for comp in range(3)]
    inner = waves[0] * velocity[0] + waves[1] * velocity[1] + waves[2] * velocity[2]
    square = jnp.maximum(waves[0] * waves[0] + waves[1] * waves[1] + waves[2] * waves[2], 1.0)
    projected = [
        jnp.where(keep, velocity[comp] - waves[comp] * inner / square, 0.0) for comp in range(3)
    ]
    stress_parts = []
    for first, second in PAIRS:
        if first == second:
            value = waves[first] * projected[first]
        else:
            value = waves[second] * projected[first] + waves[first] * projected[second]
        stress_parts.append(jnp.stack([-STEP_DT * value[1], STEP_DT * value[0]]))
    stress_hat = jnp.stack(stress_parts, axis=1)
    back_x = complex_product("cskqp,px->cskxq", stress_hat, cos_x.T / NX, sin_x.T / NX)
    stress_mid = complex_product(
        "cskxq,qy->csxyk",
        lax.all_to_all(back_x, "row", split_axis=4, concat_axis=5, tiled=True),
        cos_y.T / NY,
        sin_y.T / NY,
    )
    real_z = cos_z.T * weight_z[:, None]
    imag_z = sin_z.T * weight_z[:, None]
    part = lax.all_to_all(stress_mid, "col", split_axis=4, concat_axis=5, tiled=True)
    stress = contract("csxyk,kz->csxyz", part[0], real_z) - contract(
        "csxyk,kz->csxyz", part[1], imag_z
    )
    inputs_count = features.shape[0]
    stress_count = stress.shape[0]
    cells = stress.shape[1] * stress.shape[2] * stress.shape[3] * stress.shape[4]
    feats = features.reshape(inputs_count, cells)
    grads = stress.astype(jnp.bfloat16).reshape(stress_count, cells)
    hidden = w_mid.shape[0]
    blank = jnp.zeros((inputs_count, cells), jnp.float32)
    block = math.gcd(cells, max(1024, cells // 8))

    def visit(index, carry):
        current, totals = carry
        start = (0 + index * block).astype(jnp.int32)
        x_blk = lax.dynamic_slice_in_dim(feats, start, block, 1)
        g_blk = lax.dynamic_slice_in_dim(grads, start, block, 1)
        grad_x, parts = closure_block(x_blk, g_blk, w_in, bias_in, w_mid, bias_mid, w_out)
        current = lax.dynamic_update_slice_in_dim(current, grad_x, start, 1)
        return (current, tuple((a + b for a, b in zip(totals, parts))))

    init = (
        jnp.zeros((inputs_count, hidden), jnp.float32),
        jnp.zeros((hidden,), jnp.float32),
        jnp.zeros((hidden, hidden), jnp.float32),
        jnp.zeros((hidden,), jnp.float32),
        jnp.zeros((hidden, stress_count), jnp.float32),
    )
    field, local = lax.fori_loop(0, cells // block, visit, (blank, init))
    totals = lax.psum((local[0], local[1], local[2], local[3], local[4]), ("row", "col"))
    factor = 1.0 / math.sqrt(CELLS)
    return (
        field.reshape(features.shape),
        totals[0] * factor,
        totals[1] * factor,
        totals[2] * factor,
        totals[3] * factor,
        totals[4] * factor,
    )


def solution(mesh):
    return jax.shard_map(
        per_device,
        mesh=mesh,
        in_specs=(
            P(None, None, "row", "col", None),
            P(None, None, "row", "col", None),
            P(),
            P(),
            P(),
            P(),
            P(),
        ),
        out_specs=(P(None, None, "row", "col", None), P(), P(), P(), P(), P()),
        check_vma=False,
    )
```

profile of v0, /device:TPU:0, one launch (start us, length us, event | category | flops | bytes accessed | tf_op | source)
XLA Modules:
  0.0 856.4 jit_solution(18035341283685795229)
XLA Ops:
  10.6 6.0 copy.51
  16.6 5.9 reshape.562
  22.5 25.4 %all_to_all.60 = f32[4,1,98304]{2,1,0:T(1,128)S(1)} all-to-all(f32[4,1,98304]{2,1,0:T(1,128)} %reshape.562), channel_id=1, replica_groups=mesh['row'=8,'col'=4] {'col'}, dimensions={0} | all-to-all | bytes 3145728 | tf_op jit(solution)/shard_map/all_to_all | solution.py:82
  48.4 6.4 reduce.2
  54.7 6.3 reshape.563
  61.0 6.8 copy.95
  81.1 6.0 copy.53
  87.1 7.6 reshape.564
  94.7 5.2 all-to-all-start.1
  100.6 36.9 %all-to-all-done.1 = f32[8,1,49152]{2,1,0:T(1,128)S(1)} async-done(((f32[8,1,49152]{2,1,0:T(1,128)}), f32[8,1,49152]{2,1,0:T(1,128)S(1)}, u32[]{:S(2)}, u32[]{:S(2)}) %all-to-all-start.1) | async-done | bytes 1572896 | tf_op jit(solution)/shard_map/all_to_all | solution.py:88
  137.5 6.2 reduce.3
  143.7 6.1 reshape.565
  154.4 5.1 fusion.55
  159.5 5.5 fusion.48
  165.4 5.1 fusion.21
  170.5 5.1 fusion.20
  186.4 11.4 %copy.63 = f32[2,6,1,32,128,16]{3,5,1,2,0,4:T(8,128)} copy(f32[2,6,1,32,128,16]{4,3,5,1,2,0:T(8,128)} %pad_maximum_fusion) | data formatting | bytes 6291456 | tf_op jit(solution)/shard_map/stack | solution.py:36
  197.8 10.6 %reshape.566 = f32[8,1,98304]{2,1,0:T(1,128)} reshape(f32[128,2,1,6,16,32]{5,4,3,2,1,0:T(8,128)} %bitcast.283) | data formatting | bytes 6291456
  208.5 76.0 %all_to_all.61 = f32[8,1,98304]{2,1,0:T(1,128)} all-to-all(f32[8,1,98304]{2,1,0:T(1,128)} %reshape.566), channel_id=1, replica_groups=mesh['row'=8,'col'=4] {'row'}, dimensions={0} | all-to-all | bytes 6291456 | tf_op jit(solution)/shard_map/all_to_all | solution.py:118
  284.4 11.7 %reduce.4 = f32[8,98304]{1,0:T(8,128)} reduce(f32[8,1,98304]{2,1,0:T(1,128)} %all_to_all.61, f32[]{:T(128)} %broadcast.808), dimensions={1}, to_apply=%all_to_all.50.reduce_sub_computation | reduce | bytes 6291460 | tf_op jit(solution)/shard_map/all_to_all | solution.py:118
  296.1 10.9 %reshape.567 = f32[128,2,1,6,16,32]{5,4,3,2,1,0:T(8,128)} reshape(f32[8,98304]{1,0:T(8,128)} %reduce.4) | data formatting | bytes 6291456
  307.0 10.4 %copy.64 = f32[2,6,1,32,128,16]{3,5,4,1,0,2:T(8,128)} copy(f32[2,6,1,32,128,16]{3,5,1,2,0,4:T(8,128)} %bitcast.281) | data formatting | bytes 6291456 | tf_op jit(solution)/shard_map/all_to_all | solution.py:118
  317.4 10.7 %fusion.205 = (f32[1,6,1,32,16,8,16]{3,6,4,5,1,0,2:T(8,128)}, f32[1,6,1,32,16,8,16]{3,6,4,5,1,0,2:T(8,128)}) fusion(f32[2,6,1,32,16,8,16]{3,6,4,5,1,0,2:T(8,128)} %bitcast.279), kind=kLoop, calls=%fused_computation.273 | loop fusion | bytes 6291456 | tf_op jit(solution)/shard_map/slice | solution.py:34
  328.1 3.7 copy.65
  331.8 10.1 %fusion.64 = f32[128,6,32,16]{0,2,3,1:T(8,128)S(1)} fusion(f32[6,32,16,128]{1,3,2,0:T(8,128)S(1)} %bitcast.277, s32[128]{0:T(128)S(1)} %compare_select_fusion), kind=kOutput, calls=%fused_computation.138 | convolution fusion | flops 604225536 | bytes 3146240 | tf_op jit(solution)/shard_map/cskxq,qy->csxyk/dot_general | solution.py:28
  341.9 10.2 %fusion.43 = f32[128,6,32,16]{0,2,3,1:T(8,128)S(1)} fusion(f32[6,32,16,128]{1,3,2,0:T(8,128)S(1)} %bitcast.278, s32[128]{0:T(128)S(1)} %compare_select_fusion), kind=kOutput, calls=%fused_computation.117 | convolution fusion | flops 604225536 | bytes 3146240 | tf_op jit(solution)/shard_map/cskxq,qy->csxyk/dot_general | solution.py:28
  353.1 10.5 %subtract_bitcast_fusion = f32[1,6,1,16,128,32]{4,5,3,1,2,0:T(8,128)S(1)} fusion(f32[128,6,32,16]{0,2,3,1:T(8,128)S(1)} %fusion.64, f32[6,32,16,128]{1,3,2,0:T(8,128)S(1)} %bitcast.275, s32[128]{0:T(128)S(1)} %compare_select_fusion), kind=kOutput, calls=%fused_computation.41 | convolution fusion | flops 604618752 | bytes 4719104 | tf_op jit(solution)/shard_map/cskxq,qy->csxyk/dot_general | solution.py:28
  363.6 10.1 %add_bitcast_fusion = f32[1,6,1,16,128,32]{4,5,3,1,2,0:T(8,128)S(1)} fusion(f32[128,6,32,16]{0,2,3,1:T(8,128)S(1)} %fusion.43, f32[6,32,16,128]{1,3,2,0:T(8,128)S(1)} %bitcast.276, s32[128]{0:T(128)S(1)} %compare_select_fusion), kind=kOutput, calls=%fused_computation.40 | convolution fusion | flops 604618752 | bytes 4719104 | tf_op jit(solution)/shard_map/cskxq,qy->csxyk/dot_general | solution.py:28
  375.7 11.4 %copy.71 = f32[2,6,1,16,128,32]{5,3,1,2,0,4:T(8,128)} copy(f32[2,6,1,16,128,32]{4,5,3,1,2,0:T(8,128)} %pad_maximum_fusion.1) | data formatting | bytes 6291456 | tf_op jit(solution)/shard_map/stack | solution.py:36
  387.1 9.3 %reshape.568 = f32[4,1,196608]{2,1,0:T(1,128)} reshape(f32[128,2,1,6,16,32]{5,4,3,2,1,0:T(8,128)} %bitcast.284) | data formatting | bytes 6291456
  396.4 4.8 all-to-all-start.3
  404.2 33.1 %all-to-all-done.3 = f32[4,1,196608]{2,1,0:T(1,128)} async-done(((f32[4,1,196608]{2,1,0:T(1,128)}), f32[4,1,196608]{2,1,0:T(1,128)}, u32[]{:S(2)}, u32[]{:S(2)}) %all-to-all-start.3) | async-done | bytes 3145760 | tf_op jit(solution)/shard_map/all_to_all | solution.py:124
  437.3 11.8 %reduce.5 = f32[4,196608]{1,0:T(4,128)} reduce(f32[4,1,196608]{2,1,0:T(1,128)} %all-to-all-done.3, f32[]{:T(128)} %broadcast.808), dimensions={1}, to_apply=%all_to_all.53.reduce_sub_computation | reduce | bytes 6291460 | tf_op jit(solution)/shard_map/all_to_all | solution.py:124
  449.1 10.7 %reshape.569 = f32[128,2,1,6,16,32]{5,4,3,2,1,0:T(8,128)} reshape(f32[4,196608]{1,0:T(4,128)} %reduce.5) | data formatting | bytes 6291456
  459.9 16.4 %copy.94 = f32[2,6,1,16,4,32,32]{6,4,5,3,1,2,0:T(4,128)} copy(f32[2,6,1,16,4,32,32]{6,3,1,0,5,4,2:T(8,128)} %bitcast.282) | data formatting | bytes 6291456 | tf_op jit(solution)/shard_map/all_to_all | solution.py:124
  476.3 14.3 %fusion.204 = (f32[1,6,1,16,32,4,32]{6,5,4,3,1,2,0:T(4,128)}, f32[1,6,1,16,32,4,32]{6,5,4,3,1,2,0:T(4,128)}) fusion(f32[2,6,1,16,32,4,32]{6,5,4,3,1,2,0:T(4,128)} %bitcast.280), kind=kLoop, calls=%fused_computation.272 | loop fusion | bytes 6291456 | tf_op jit(solution)/shard_map/slice | solution.py:126
  490.7 6.0 reshape.552
  499.7 5.8 reshape.553
  511.5 165.8 %while.24 = (s32[]{:T(128)}, f32[9,65536]{1,0:T(8,128)}, f32[9,256]{1,0:T(8,128)S(1)}, f32[256]{0:T(256)S(1)}, f32[256,256]{1,0:T(8,128)S(1)}, /*index=5*/f32[25...) while((s32[]{:T(128)}, f32[9,65536]{1,0:T(8,128)}, ...), condition=%wide.region_3.4_spmd.clone, body=%wide.region_0.3_spmd.clone.sunk | while | flops 3422691328 | bytes 157343136 | solution.py:153
  517.5 3.9 convert_reduce_fusion.5
  521.4 4.3 fusion.269
  538.2 3.9 convert_reduce_fusion.5
  542.1 4.4 fusion.269
  546.5 3.7 convolution_add_fusion.11
  558.9 3.9 convert_reduce_fusion.5
  562.8 4.4 fusion.269
  567.2 3.7 convolution_add_fusion.11
  579.6 3.9 convert_reduce_fusion.5
  583.5 4.3 fusion.269
  587.9 3.7 convolution_add_fusion.11
  600.2 3.9 convert_reduce_fusion.5
  604.2 4.4 fusion.269
  608.6 3.7 convolution_add_fusion.11
  621.0 3.9 convert_reduce_fusion.5
  624.9 4.4 fusion.269
  629.3 3.7 convolution_add_fusion.11
  641.6 3.9 convert_reduce_fusion.5
  645.6 4.3 fusion.269
  650.0 3.7 convolution_add_fusion.11
  662.3 3.9 convert_reduce_fusion.5
  666.3 4.3 fusion.269
  670.6 3.7 convolution_add_fusion.11
  677.3 37.5 %all-reduce = (f32[9,256]{1,0:T(8,128)S(1)}, f32[256]{0:T(256)S(1)}, f32[256]{0:T(256)S(1)}, f32[256,6]{0,1:T(8,128)S(1)}) all-reduce(f32[9,256]{1,0:T(8,128)S(1)} %get-tuple-element.241, f32[256]{0:T(256)S(1)} %get-tuple-element.242, f32[256]{0:T(256)S(1)} %get-tuple-element.244, ...), channel_id=1, replica_groups=mesh['row'=8,'col'=4] {'row','col'}, use_global_device_ids=true, to_apply=%region_4.5 | all-reduce | flops 4352 | bytes 34816 | tf_op jit(solution)/shard_map/psum | solution.py:154
  721.8 125.8 %all-reduce.3.cloned.1.call-done = f32[256,256]{1,0:T(8,128)} async-done(((f32[256,256]{1,0:T(8,128)}), f32[256,256]{1,0:T(8,128)}) %all-reduce.3.cloned.1.call-update) | async-done | bytes 262160 | tf_op jit(solution)/shard_map/psum | solution.py:154
  (236 shorter events, 129.4 us)
Async XLA Ops:
  7.2 1.1 copy-start
  94.7 42.8 %all-to-all-start.1 = ((f32[8,1,49152]{2,1,0:T(1,128)}), f32[8,1,49152]{2,1,0:T(1,128)S(1)}, u32[]{:S(2)}, u32[]{:S(2)}) async-start(f32[8,1,49152]{2,1,0:T(1,128)} %reshape.564), calls=%async_computation.1 | async-start | bytes 3145728 | tf_op jit(solution)/shard_map/all_to_all | solution.py:88
  331.8 20.3 %slice-start = ((s8[6291456]{0:T(1024)(128)(4,1)}), s8[4194304]{0:T(1024)(128)(4,1)S(1)}, s32[]{:S(2)}) async-start(s8[6291456]{0:T(1024)(128)(4,1)} %bitcast.291), calls=%async_computation.5 | async-start | bytes 8388608
  341.9 10.3 %slice-start.1 = ((s8[6291456]{0:T(1024)(128)(4,1)}), s8[2097152]{0:T(1024)(128)(4,1)S(1)}, s32[]{:S(2)}) async-start(s8[6291456]{0:T(1024)(128)(4,1)} %bitcast.291), calls=%async_computation.6 | async-start | bytes 4194304
  396.4 4.9 copy-start.9
  396.4 40.9 %all-to-all-start.3 = ((f32[4,1,196608]{2,1,0:T(1,128)}), f32[4,1,196608]{2,1,0:T(1,128)}, u32[]{:S(2)}, u32[]{:S(2)}) async-start(f32[4,1,196608]{2,1,0:T(1,128)} %reshape.568), calls=%async_computation.3 | async-start | bytes 6291456 | tf_op jit(solution)/shard_map/all_to_all | solution.py:124
  401.2 446.4 %all-reduce.3.cloned.1.call-start = ((), (), s32[]{:S(2)}) async-start(), calls=%async_computation.4 | async-start | bytes 524288 | tf_op jit(solution)/shard_map/psum | solution.py:154
  508.6 2.8 copy-start.10
  508.7 2.8 copy-start.11
  508.7 2.8 copy-start.12
  508.7 2.8 copy-start.13
  508.7 2.8 copy-start.14
  514.1 3.4 copy-start.3
  515.4 2.1 copy-start.6
  517.5 4.0 copy-start.5
  521.4 4.4 copy-start.4
  525.8 3.7 copy-start.2
  529.5 2.3 copy-start.7
  534.8 3.4 copy-start.3
  536.1 2.1 copy-start.6
  538.2 4.0 copy-start.5
  542.1 4.4 copy-start.4
  546.5 3.7 copy-start.2
  550.2 2.3 copy-start.7
  555.5 3.4 copy-start.3
  556.8 2.1 copy-start.6
  558.8 4.0 copy-start.5
  562.8 4.4 copy-start.4
  567.2 3.7 copy-start.2
  570.9 2.3 copy-start.7
  576.2 3.4 copy-start.3
  577.5 2.1 copy-start.6
  579.5 4.0 copy-start.5
  583.5 4.4 copy-start.4
  587.9 3.7 copy-start.2
  591.6 2.3 copy-start.7
  596.9 3.4 copy-start.3
  598.1 2.1 copy-start.6
  600.2 4.0 copy-start.5
  604.2 4.4 copy-start.4
  608.6 3.7 copy-start.2
  612.3 2.3 copy-start.7
  617.6 3.4 copy-start.3
  618.9 2.1 copy-start.6
  620.9 4.0 copy-start.5
  624.9 4.4 copy-start.4
  629.3 3.7 copy-start.2
  633.0 2.3 copy-start.7
  638.3 3.3 copy-start.3
  639.6 2.1 copy-start.6
  641.6 4.0 copy-start.5
  645.6 4.4 copy-start.4
  650.0 3.7 copy-start.2
  653.7 2.3 copy-start.7
  659.0 3.4 copy-start.3
  660.2 2.1 copy-start.6
  662.3 4.0 copy-start.5
  666.3 4.3 copy-start.4
  670.6 3.7 copy-start.2
  674.3 2.3 copy-start.7
  677.3 42.4 %copy-start.8 = (f32[256,256]{1,0:T(8,128)}, f32[256,256]{1,0:T(8,128)S(1)}, u32[]{:S(2)}) copy-start(f32[256,256]{1,0:T(8,128)S(1)} %get-tuple-element.243) | copy-start | bytes 786436
  716.5 132.8 %copy-start.1 = (f32[3,1,16,32,128]{4,3,2,1,0:T(8,128)S(1)}, f32[3,1,16,32,128]{4,3,2,1,0:T(8,128)}, u32[]{:S(2)}) copy-start(f32[3,1,16,32,128]{4,3,2,1,0:T(8,128)} %param.10) | copy-start | bytes 2359300
Sparse Core Ops, SparseCore 0:
  721.3 126.2 all-reduce.2
where the time goes:
time: 862 us; the launch traced here: 856 us
  matrix products  242 us (28%)
  local copies, waits for them, and re-layouts  207 us (24%)
  waiting for transfers between devices  196 us (23%)
  blocking collectives  139 us (16%)
  other arithmetic  46.9 us (5%)
  between operations  14.9 us (2%)
  starting transfers between devices  9.97 us (1%)
    psum x1, waiting for transfers between devices, per_device(): lax.psum((local[0], local[1], local[2], local[3], local[4]), ('row', 'col'))  126 us
    dot_general x20, matrix products, contract(): jnp.einsum(form, left, right, precision=lax.Precision.HIGHEST, preferred_...  81.1 us
    unnamed x35, local copies, waits for them, and re-layouts  76.7 us
    all_to_all x1, blocking collectives, per_device(): lax.all_to_all(back_x, 'row', split_axis=4, concat_axis=5, tiled=True)  76 us
    psum x1, blocking collectives, per_device(): lax.psum((local[0], local[1], local[2], local[3], local[4]), ('row', 'col'))  37.5 us
    all_to_all x1, waiting for transfers between devices, per_device(): lax.all_to_all(spectra, 'row', split_axis=4, concat_axis=5, tiled=True)  36.9 us
    dot_general x8, matrix products, closure_block(): jnp.einsum('fh,hn->fn', w_in, delta_in, preferred_element_type=jnp.float32)  34.8 us
    all_to_all x1, waiting for transfers between devices, per_device(): lax.all_to_all(stress_mid, 'col', split_axis=4, concat_axis=5, tiled=True)  33.1 us
  transfers between devices with their start and end apart: 3, of which 3 were waited for; matrix products, arithmetic and copies ran while one was open for 0% of the time, Pallas kernels for 0%

commit v1 on v0

--- a/solution.py
+++ b/solution.py
@@ -10,6 +10,28 @@
 CELLS = 2097152
 STEP_DT = 0.04
 PAIRS = ((0, 0), (1, 1), (2, 2), (0, 1), (0, 2), (1, 2))
+
+
+def detail_view_over_axis(u_in):
+    axis_key = "row"
+    response = lax.axis_size(axis_key)
+    kept_arr = lax.axis_index(axis_key)
+    arr_out, k_now = (response, kept_arr)
+    vec_out = u_in.shape[4] // arr_out
+    item_now = list(u_in.shape)
+    item_now[4] = vec_out
+    fresh = item_now[5]
+    item_now[5] = fresh * arr_out
+    f_next = jnp.zeros(item_now, u_in.dtype)
+    for rr in tuple(range(arr_out)):
+        spare = lax.dynamic_slice_in_dim(u_in, (k_now ^ rr) * vec_out, vec_out, axis=4)
+        if rr:
+            leaves = []
+            for p in tuple(range(arr_out)):
+                leaves.append((p, p ^ rr))
+            spare = lax.ppermute(spare, axis_name=axis_key, perm=leaves)
+        f_next = lax.dynamic_update_slice_in_dim(f_next, spare, (k_now ^ rr) * fresh, axis=5)
+    return f_next
 
 
 def mode_list(count, length):
@@ -114,10 +136,7 @@
     stress_hat = jnp.stack(stress_parts, axis=1)
     back_x = complex_product("cskqp,px->cskxq", stress_hat, cos_x.T / NX, sin_x.T / NX)
     stress_mid = complex_product(
-        "cskxq,qy->csxyk",
-        lax.all_to_all(back_x, "row", split_axis=4, concat_axis=5, tiled=True),
-        cos_y.T / NY,
-        sin_y.T / NY,
+        "cskxq,qy->csxyk", detail_view_over_axis(back_x), cos_y.T / NY, sin_y.T / NY
     )
     real_z = cos_z.T * weight_z[:, None]
     imag_z = sin_z.T * weight_z[:, None]

time: 862 us -> 1070 us (1.24)
  local copies, waits for them, and re-layouts: 207 us -> 455 us
  blocking collectives: 139 us -> 62.5 us
  waiting for transfers between devices: 196 us -> 257 us
  matrix products: 242 us -> 209 us
    dynamic_update_slice x0 -> x8, local copies, waits for them, and re-layouts: none -> 254 us  [detail_view_over_axis(): lax.dynamic_update_slice_in_dim(f_next, spare, (k_now ^ rr) * fresh, axis=5)]
    all_to_all x1 -> x0, blocking collectives: 76 us -> none  [per_device(): lax.all_to_all(back_x, 'row', split_axis=4, concat_axis=5, tiled=True)]
    ppermute x0 -> x7, waiting for transfers between devices: none -> 59.5 us  [detail_view_over_axis(): spare = lax.ppermute(spare, axis_name=axis_key, perm=leaves)]
    dot_general x20, matrix products: 81.1 us -> 48.8 us  [contract(): jnp.einsum(form, left, right, precision=lax.Precision.HIGHEST, preferred_...]
    dynamic_slice x0 -> x8, local copies, waits for them, and re-layouts: none -> 27.4 us  [detail_view_over_axis(): lax.dynamic_slice_in_dim(u_in, (k_now ^ rr) * vec_out, vec_out, axis=4)]
    ppermute x0 -> x7, local copies, waits for them, and re-layouts: none -> 23 us  [detail_view_over_axis(): spare = lax.ppermute(spare, axis_name=axis_key, perm=leaves)]
    unnamed x35 -> x33, local copies, waits for them, and re-layouts: 76.7 us -> 55.2 us
    another operation x3 -> x4, other arithmetic: 4.14 us -> 18.2 us  [complex_product(): return jnp.stack([real, imag])]
  transfers between devices with their start and end apart: 3 -> 10, of which waited for: 3 -> 4; matrix products, arithmetic and copies ran while one was open for 0% -> 26% of each run, Pallas kernels for 0% -> 0%
where the time goes in v1:
time: 1070 us
  local copies, waits for them, and re-layouts  455 us (43%)
  waiting for transfers between devices  257 us (24%)
  matrix products  209 us (20%)
  blocking collectives  62.5 us (6%)
  other arithmetic  49.2 us (5%)
  starting transfers between devices  17.1 us (2%)
  between operations  15 us (1%)
    dynamic_update_slice x8, local copies, waits for them, and re-layouts, detail_view_over_axis(): lax.dynamic_update_slice_in_dim(f_next, spare, (k_now ^ rr) * fresh, axis=5)  254 us
    psum x1, waiting for transfers between devices, per_device(): lax.psum((local[0], local[1], local[2], local[3], local[4]), ('row', 'col'))  126 us
    ppermute x7, waiting for transfers between devices, detail_view_over_axis(): spare = lax.ppermute(spare, axis_name=axis_key, perm=leaves)  59.5 us
    unnamed x33, local copies, waits for them, and re-layouts  55.2 us
    dot_general x20, matrix products, contract(): jnp.einsum(form, left, right, precision=lax.Precision.HIGHEST, preferred_...  48.8 us
    psum x1, blocking collectives, per_device(): lax.psum((local[0], local[1], local[2], local[3], local[4]), ('row', 'col'))  37.1 us
    all_to_all x1, waiting for transfers between devices, per_device(): lax.all_to_all(spectra, 'row', split_axis=4, concat_axis=5, tiled=True)  36.9 us
    dot_general x8, matrix products, closure_block(): jnp.einsum('fh,hn->fn', w_in, delta_in, preferred_element_type=jnp.float32)  34.8 us
  transfers between devices with their start and end apart: 10, of which 4 were waited for; matrix products, arithmetic and copies ran while one was open for 26% of the time, Pallas kernels for 0%

profile of v1, /device:TPU:0, one launch (start us, length us, event | category | flops | bytes accessed | tf_op | source)
XLA Modules:
  0.0 1065.7 jit_solution(1423638632013207820)
XLA Ops:
  10.6 6.0 copy.58
  16.6 5.9 reshape.558
  22.5 25.4 %all_to_all.45 = f32[4,1,98304]{2,1,0:T(1,128)S(1)} all-to-all(f32[4,1,98304]{2,1,0:T(1,128)} %reshape.558), channel_id=1, replica_groups=mesh['row'=8,'col'=4] {'col'}, dimensions={0} | all-to-all | bytes 3145728 | tf_op jit(solution)/shard_map/all_to_all | solution.py:104
  48.4 6.4 reduce.2
  54.8 6.2 reshape.559
  61.0 6.8 copy.105
  81.1 6.0 copy.60
  87.1 7.6 reshape.560
  94.8 5.2 all-to-all-start.1
  100.7 36.9 %all-to-all-done.1 = f32[8,1,49152]{2,1,0:T(1,128)S(1)} async-done(((f32[8,1,49152]{2,1,0:T(1,128)}), f32[8,1,49152]{2,1,0:T(1,128)S(1)}, u32[]{:S(2)}, u32[]{:S(2)}) %all-to-all-start.1) | async-done | bytes 1572896 | tf_op jit(solution)/shard_map/all_to_all | solution.py:110
  137.6 6.2 reduce.3
  143.7 6.1 reshape.561
  154.4 5.1 fusion.64
  159.5 5.5 fusion.57
  165.4 5.1 fusion.31
  170.5 5.1 fusion.30
  184.4 9.9 fusion.15
  201.1 6.2 fusion.22
  228.4 59.5 %collective-permute-done.1 = f32[2,6,1,32,16,16]{3,5,4,2,1,0:T(8,128)} collective-permute-done((f32[2,6,1,32,16,16]{3,5,4,2,1,0:T(8,128)}, f32[2,6,1,32,16,16]{3,5,4,2,1,0:T(8,128)}, u32[]{:S(2)}, u32[]{:S(2)}) %collective-permute-start.1) | collective-permute-done | bytes 393248 | tf_op jit(solution)/shard_map/ppermute | solution.py:32
  289.3 5.2 copy.70
  296.6 16.0 %dynamic_update_slice.31 = f32[2,6,1,32,16,128]{5,3,4,1,2,0:T(8,128)} dynamic-update-slice(f32[2,6,1,32,16,128]{5,3,4,1,2,0:T(8,128)} %broadcast_in_dim.30, f32[2,6,1,32,16,16]{5,3,4,1,2,0:T(8,128)} %copy.70, s32[]{:T(128)} %constant.104.clone.1, s32[]{:T(128)} %constant.104.clone.1, s32[]{:T(128)} %constant.104.clone.1, s32[]{:T(128)} %constant.104.clone.1, s32[]{:T(128)} %constant.104.clone.1, ...) | dynamic-update-slice | bytes 786436 | tf_op jit(solution)/shard_map/dynamic_update_slice | solution.py:33
  315.9 33.9 %dynamic_update_slice.32 = f32[2,6,1,32,16,128]{5,3,4,1,2,0:T(8,128)} dynamic-update-slice(f32[2,6,1,32,16,128]{5,3,4,1,2,0:T(8,128)} %dynamic_update_slice.31, f32[2,6,1,32,16,16]{5,3,4,1,2,0:T(8,128)} %copy.72, s32[]{:T(128)} %constant.104.clone.1, s32[]{:T(128)} %constant.104.clone.1, s32[]{:T(128)} %constant.104.clone.1, s32[]{:T(128)} %constant.104.clone.1, s32[]{:T(128)} %constant.104.clone.1, ...) | dynamic-update-slice | bytes 786436 | tf_op jit(solution)/shard_map/dynamic_update_slice | solution.py:33
  353.1 33.9 %dynamic_update_slice.33 = f32[2,6,1,32,16,128]{5,3,4,1,2,0:T(8,128)} dynamic-update-slice(f32[2,6,1,32,16,128]{5,3,4,1,2,0:T(8,128)} %dynamic_update_slice.32, f32[2,6,1,32,16,16]{5,3,4,1,2,0:T(8,128)} %copy.74, s32[]{:T(128)} %constant.104.clone.1, s32[]{:T(128)} %constant.104.clone.1, s32[]{:T(128)} %constant.104.clone.1, s32[]{:T(128)} %constant.104.clone.1, s32[]{:T(128)} %constant.104.clone.1, ...) | dynamic-update-slice | bytes 786436 | tf_op jit(solution)/shard_map/dynamic_update_slice | solution.py:33
  390.3 33.9 %dynamic_update_slice.34 = f32[2,6,1,32,16,128]{5,3,4,1,2,0:T(8,128)} dynamic-update-slice(f32[2,6,1,32,16,128]{5,3,4,1,2,0:T(8,128)} %dynamic_update_slice.33, f32[2,6,1,32,16,16]{5,3,4,1,2,0:T(8,128)} %copy.76, s32[]{:T(128)} %constant.104.clone.1, s32[]{:T(128)} %constant.104.clone.1, s32[]{:T(128)} %constant.104.clone.1, s32[]{:T(128)} %constant.104.clone.1, s32[]{:T(128)} %constant.104.clone.1, ...) | dynamic-update-slice | bytes 786436 | tf_op jit(solution)/shard_map/dynamic_update_slice | solution.py:33
  427.5 33.9 %dynamic_update_slice.35 = f32[2,6,1,32,16,128]{5,3,4,1,2,0:T(8,128)} dynamic-update-slice(f32[2,6,1,32,16,128]{5,3,4,1,2,0:T(8,128)} %dynamic_update_slice.34, f32[2,6,1,32,16,16]{5,3,4,1,2,0:T(8,128)} %copy.78, s32[]{:T(128)} %constant.104.clone.1, s32[]{:T(128)} %constant.104.clone.1, s32[]{:T(128)} %constant.104.clone.1, s32[]{:T(128)} %constant.104.clone.1, s32[]{:T(128)} %constant.104.clone.1, ...) | dynamic-update-slice | bytes 786436 | tf_op jit(solution)/shard_map/dynamic_update_slice | solution.py:33
  464.7 33.9 %dynamic_update_slice.36 = f32[2,6,1,32,16,128]{5,3,4,1,2,0:T(8,128)} dynamic-update-slice(f32[2,6,1,32,16,128]{5,3,4,1,2,0:T(8,128)} %dynamic_update_slice.35, f32[2,6,1,32,16,16]{5,3,4,1,2,0:T(8,128)} %copy.80, s32[]{:T(128)} %constant.104.clone.1, s32[]{:T(128)} %constant.104.clone.1, s32[]{:T(128)} %constant.104.clone.1, s32[]{:T(128)} %constant.104.clone.1, s32[]{:T(128)} %constant.104.clone.1, ...) | dynamic-update-slice | bytes 786436 | tf_op jit(solution)/shard_map/dynamic_update_slice | solution.py:33
  501.9 33.9 %dynamic_update_slice.37 = f32[2,6,1,32,16,128]{5,3,4,1,2,0:T(8,128)} dynamic-update-slice(f32[2,6,1,32,16,128]{5,3,4,1,2,0:T(8,128)} %dynamic_update_slice.36, f32[2,6,1,32,16,16]{5,3,4,1,2,0:T(8,128)} %copy.82, s32[]{:T(128)} %constant.104.clone.1, s32[]{:T(128)} %constant.104.clone.1, s32[]{:T(128)} %constant.104.clone.1, s32[]{:T(128)} %constant.104.clone.1, s32[]{:T(128)} %constant.104.clone.1, ...) | dynamic-update-slice | bytes 786436 | tf_op jit(solution)/shard_map/dynamic_update_slice | solution.py:33
  539.1 34.3 %dynamic_update_slice.38 = f32[2,6,1,32,16,128]{5,3,4,1,2,0:T(8,128)} dynamic-update-slice(f32[2,6,1,32,16,128]{5,3,4,1,2,0:T(8,128)} %dynamic_update_slice.37, f32[2,6,1,32,16,16]{5,3,4,1,2,0:T(8,128)} %copy.84, s32[]{:T(128)} %constant.104.clone.1, s32[]{:T(128)} %constant.104.clone.1, s32[]{:T(128)} %constant.104.clone.1, s32[]{:T(128)} %constant.104.clone.1, s32[]{:T(128)} %constant.104.clone.1, ...) | dynamic-update-slice | bytes 786436 | tf_op jit(solution)/shard_map/dynamic_update_slice | solution.py:33
  584.0 11.4 %copy.85 = f32[2,6,1,16,128,32]{5,3,1,2,0,4:T(8,128)} copy(f32[2,6,1,16,128,32]{4,5,3,1,2,0:T(8,128)} %pad_maximum_fusion) | data formatting | bytes 6291456 | tf_op jit(solution)/shard_map/stack | solution.py:58
  595.4 9.3 reshape.562
  604.7 4.8 all-to-all-start.2
  612.5 34.2 %all-to-all-done.2 = f32[4,1,196608]{2,1,0:T(1,128)} async-done(((f32[4,1,196608]{2,1,0:T(1,128)}), f32[4,1,196608]{2,1,0:T(1,128)}, u32[]{:S(2)}, u32[]{:S(2)}) %all-to-all-start.2) | async-done | bytes 3145760 | tf_op jit(solution)/shard_map/all_to_all | solution.py:143
  646.7 11.8 %reduce.4 = f32[4,196608]{1,0:T(4,128)} reduce(f32[4,1,196608]{2,1,0:T(1,128)} %all-to-all-done.2, f32[]{:T(128)} %broadcast.808), dimensions={1}, to_apply=%all_to_all.39.reduce_sub_computation | reduce | bytes 6291460 | tf_op jit(solution)/shard_map/all_to_all | solution.py:143
  658.6 10.8 %reshape.563 = f32[128,2,1,6,16,32]{5,4,3,2,1,0:T(8,128)} reshape(f32[4,196608]{1,0:T(4,128)} %reduce.4) | data formatting | bytes 6291456
  669.3 16.4 %copy.104 = f32[2,6,1,16,4,32,32]{6,4,5,3,1,2,0:T(4,128)} copy(f32[2,6,1,16,4,32,32]{6,3,1,0,5,4,2:T(8,128)} %bitcast.273) | data formatting | bytes 6291456 | tf_op jit(solution)/shard_map/all_to_all | solution.py:143
  685.8 14.4 %fusion.212 = (f32[1,6,1,16,32,4,32]{6,5,4,3,1,2,0:T(4,128)}, f32[1,6,1,16,32,4,32]{6,5,4,3,1,2,0:T(4,128)}) fusion(f32[2,6,1,16,32,4,32]{6,5,4,3,1,2,0:T(4,128)} %bitcast.272), kind=kLoop, calls=%fused_computation.297 | loop fusion | bytes 6291456 | tf_op jit(solution)/shard_map/slice | solution.py:145
  700.2 6.0 reshape.548
  709.3 5.8 reshape.549
  721.0 165.9 %while.24 = (s32[]{:T(128)}, f32[9,65536]{1,0:T(8,128)}, f32[9,256]{1,0:T(8,128)S(1)}, f32[256]{0:T(256)S(1)}, f32[256,256]{1,0:T(8,128)S(1)}, /*index=5*/f32[25...) while((s32[]{:T(128)}, f32[9,65536]{1,0:T(8,128)}, ...), condition=%wide.region_3.4_spmd.clone, body=%wide.region_0.3_spmd.clone.sunk | while | flops 3422691328 | bytes 157343136 | solution.py:172
  727.0 3.9 convert_reduce_fusion.5
  731.0 4.3 fusion.272
  735.3 3.7 convolution_add_fusion.11
  747.7 3.9 convert_reduce_fusion.5
  751.7 4.3 fusion.272
  756.0 3.7 convolution_add_fusion.11
  768.4 3.9 convert_reduce_fusion.5
  772.4 4.3 fusion.272
  776.7 3.7 convolution_add_fusion.11
  789.1 3.9 convert_reduce_fusion.5
  793.1 4.3 fusion.272
  797.4 3.7 convolution_add_fusion.11
  809.8 3.9 convert_reduce_fusion.5
  813.8 4.4 fusion.272
  818.1 3.7 convolution_add_fusion.11
  830.5 3.9 convert_reduce_fusion.5
  834.5 4.4 fusion.272
  851.3 3.9 convert_reduce_fusion.5
  855.2 4.3 fusion.272
  859.6 3.7 convolution_add_fusion.11
  871.9 3.9 convert_reduce_fusion.5
  875.9 4.3 fusion.272
  880.2 3.7 convolution_add_fusion.11
  886.9 37.1 %all-reduce = (f32[9,256]{1,0:T(8,128)S(1)}, f32[256]{0:T(256)S(1)}, f32[256]{0:T(256)S(1)}, f32[256,6]{0,1:T(8,128)S(1)}) all-reduce(f32[9,256]{1,0:T(8,128)S(1)} %get-tuple-element.241, f32[256]{0:T(256)S(1)} %get-tuple-element.242, f32[256]{0:T(256)S(1)} %get-tuple-element.244, ...), channel_id=1, replica_groups=mesh['row'=8,'col'=4] {'row','col'}, use_global_device_ids=true, to_apply=%region_4.5 | all-reduce | flops 4352 | bytes 34816 | tf_op jit(solution)/shard_map/psum | solution.py:173
  931.0 125.9 %all-reduce.3.cloned.1.call-done = f32[256,256]{1,0:T(8,128)} async-done(((f32[256,256]{1,0:T(8,128)}), f32[256,256]{1,0:T(8,128)}) %all-reduce.3.cloned.1.call-update) | async-done | bytes 262160 | tf_op jit(solution)/shard_map/psum | solution.py:173
  (265 shorter events, 189.5 us)
Async XLA Ops:
  94.8 42.8 %all-to-all-start.1 = ((f32[8,1,49152]{2,1,0:T(1,128)}), f32[8,1,49152]{2,1,0:T(1,128)S(1)}, u32[]{:S(2)}, u32[]{:S(2)}) async-start(f32[8,1,49152]{2,1,0:T(1,128)} %reshape.560), calls=%async_computation.1 | async-start | bytes 3145728 | tf_op jit(solution)/shard_map/all_to_all | solution.py:110
  184.4 9.9 copy-start.9
  197.6 26.3 %collective-permute-start = (f32[2,6,1,32,16,16]{3,5,4,2,1,0:T(8,128)}, f32[2,6,1,32,16,16]{3,5,4,2,1,0:T(8,128)}, u32[]{:S(2)}, u32[]{:S(2)}) collective-permute-start(f32[2,6,1,32,16,16]{3,5,4,2,1,0:T(8,128)} %copy.71), channel_id=1, source_target_pairs={{0,4},{4,0},{8,12},{12,8},{16,20},{20,16},{24,28},{28,24},{1,5},{5... | collective-permute-start | bytes 1179656 | tf_op jit(solution)/shard_map/ppermute | solution.py:32
  201.0 86.9 %collective-permute-start.1 = (f32[2,6,1,32,16,16]{3,5,4,2,1,0:T(8,128)}, f32[2,6,1,32,16,16]{3,5,4,2,1,0:T(8,128)}, u32[]{:S(2)}, u32[]{:S(2)}) collective-permute-start(f32[2,6,1,32,16,16]{3,5,4,2,1,0:T(8,128)} %copy.73), channel_id=1, source_target_pairs={{0,8},{4,12},{8,0},{12,4},{16,24},{20,28},{24,16},{28,20},{1,9},{5... | collective-permute-start | bytes 1179656 | tf_op jit(solution)/shard_map/ppermute | solution.py:32
  213.0 174.0 %collective-permute-start.2 = (f32[2,6,1,32,16,16]{3,5,4,2,1,0:T(8,128)}, f32[2,6,1,32,16,16]{3,5,4,2,1,0:T(8,128)}, u32[]{:S(2)}, u32[]{:S(2)}) collective-permute-start(f32[2,6,1,32,16,16]{3,5,4,2,1,0:T(8,128)} %copy.75), channel_id=1, source_target_pairs={{0,12},{4,8},{8,4},{12,0},{16,28},{20,24},{24,20},{28,16},{1,13},{... | collective-permute-start | bytes 1179656 | tf_op jit(solution)/shard_map/ppermute | solution.py:32
  218.0 206.1 %collective-permute-start.3 = (f32[2,6,1,32,16,16]{3,5,4,2,1,0:T(8,128)}, f32[2,6,1,32,16,16]{3,5,4,2,1,0:T(8,128)}, u32[]{:S(2)}, u32[]{:S(2)}) collective-permute-start(f32[2,6,1,32,16,16]{3,5,4,2,1,0:T(8,128)} %copy.77), channel_id=1, source_target_pairs={{0,16},{4,20},{8,24},{12,28},{16,0},{20,4},{24,8},{28,12},{1,17},{... | collective-permute-start | bytes 1179656 | tf_op jit(solution)/shard_map/ppermute | solution.py:32
  218.2 243.2 %collective-permute-start.4 = (f32[2,6,1,32,16,16]{3,5,4,2,1,0:T(8,128)S(1)}, f32[2,6,1,32,16,16]{3,5,4,2,1,0:T(8,128)}, u32[]{:S(2)}, u32[]{:S(2)}) collective-permute-start(f32[2,6,1,32,16,16]{3,5,4,2,1,0:T(8,128)S(1)} %copy.79), channel_id=1, source_target_pairs={{0,20},{4,16},{8,28},{12,24},{16,4},{20,0},{24,12},{28,8},{1,21},{... | collective-permute-start | bytes 1179656 | tf_op jit(solution)/shard_map/ppermute | solution.py:32
  223.9 274.7 %collective-permute-start.5 = (f32[2,6,1,32,16,16]{3,5,4,2,1,0:T(8,128)}, f32[2,6,1,32,16,16]{3,5,4,2,1,0:T(8,128)}, u32[]{:S(2)}, u32[]{:S(2)}) collective-permute-start(f32[2,6,1,32,16,16]{3,5,4,2,1,0:T(8,128)} %copy.81), channel_id=1, source_target_pairs={{0,24},{4,28},{8,16},{12,20},{16,8},{20,12},{24,0},{28,4},{1,25},{... | collective-permute-start | bytes 1179656 | tf_op jit(solution)/shard_map/ppermute | solution.py:32
  287.9 247.9 %collective-permute-start.6 = (f32[2,6,1,32,16,16]{3,5,4,2,1,0:T(8,128)}, f32[2,6,1,32,16,16]{3,5,4,2,1,0:T(8,128)}, u32[]{:S(2)}, u32[]{:S(2)}) collective-permute-start(f32[2,6,1,32,16,16]{3,5,4,2,1,0:T(8,128)} %copy.83), channel_id=1, source_target_pairs={{0,28},{4,24},{8,20},{12,16},{16,12},{20,8},{24,4},{28,0},{1,29},{... | collective-permute-start | bytes 1179656 | tf_op jit(solution)/shard_map/ppermute | solution.py:32
  573.4 3.3 copy-start.8
  604.7 4.9 copy-start.11
  604.7 42.0 %all-to-all-start.2 = ((f32[4,1,196608]{2,1,0:T(1,128)}), f32[4,1,196608]{2,1,0:T(1,128)}, u32[]{:S(2)}, u32[]{:S(2)}) async-start(f32[4,1,196608]{2,1,0:T(1,128)} %reshape.562), calls=%async_computation.2 | async-start | bytes 6291456 | tf_op jit(solution)/shard_map/all_to_all | solution.py:143
  609.5 447.4 %all-reduce.3.cloned.1.call-start = ((), (), s32[]{:S(2)}) async-start(), calls=%async_computation.3 | async-start | bytes 524288 | tf_op jit(solution)/shard_map/psum | solution.py:173
  718.2 2.8 copy-start.12
  718.2 2.8 copy-start.13
  718.2 2.8 copy-start.14
  718.2 2.8 copy-start.15
  718.2 2.8 copy-start.16
  723.7 3.3 copy-start.3
  727.0 4.0 copy-start.5
  731.0 4.4 copy-start.4
  735.3 3.7 copy-start.2
  739.0 2.3 copy-start.7
  744.3 3.4 copy-start.3
  745.6 2.1 copy-start.6
  747.7 4.0 copy-start.5
  751.7 4.4 copy-start.4
  756.0 3.7 copy-start.2
  759.7 2.3 copy-start.7
  765.0 3.4 copy-start.3
  766.3 2.1 copy-start.6
  768.4 4.0 copy-start.5
  772.4 4.4 copy-start.4
  776.7 3.7 copy-start.2
  780.4 2.3 copy-start.7
  785.7 3.4 copy-start.3
  789.1 4.0 copy-start.5
  793.1 4.4 copy-start.4
  797.4 3.7 copy-start.2
  801.1 2.3 copy-start.7
  806.4 3.4 copy-start.3
  807.7 2.1 copy-start.6
  809.8 4.0 copy-start.5
  813.8 4.4 copy-start.4
  818.1 3.7 copy-start.2
  821.9 2.3 copy-start.7
  827.2 3.4 copy-start.3
  830.5 4.0 copy-start.5
  834.5 4.4 copy-start.4
  838.9 3.7 copy-start.2
  842.6 2.3 copy-start.7
  847.9 3.4 copy-start.3
  849.2 2.1 copy-start.6
  851.2 4.0 copy-start.5
  855.2 4.3 copy-start.4
  859.6 3.7 copy-start.2
  863.3 2.3 copy-start.7
  868.6 3.4 copy-start.3
  871.9 4.0 copy-start.5
  875.9 4.4 copy-start.4
  880.2 3.7 copy-start.2
  884.0 2.3 copy-start.7
  886.9 42.0 %copy-start.10 = (f32[256,256]{1,0:T(8,128)}, f32[256,256]{1,0:T(8,128)S(1)}, u32[]{:S(2)}) copy-start(f32[256,256]{1,0:T(8,128)S(1)} %get-tuple-element.243) | copy-start | bytes 786436
  925.8 132.8 %copy-start.1 = (f32[3,1,16,32,128]{4,3,2,1,0:T(8,128)S(1)}, f32[3,1,16,32,128]{4,3,2,1,0:T(8,128)}, u32[]{:S(2)}) copy-start(f32[3,1,16,32,128]{4,3,2,1,0:T(8,128)} %param.10) | copy-start | bytes 2359300
  (5 other events, 9.4 us)
Sparse Core Ops, SparseCore 0:
  930.6 126.2 all-reduce.2
